TPU v7x, 128 devices: a whole 4x4x4 slice. The times are simulated.
128 devices in a mesh: sub: 128 (over z, x, y, core).
Axes of the slice: x: 4, y: 4, z: 4, core: 2. Of those that a mesh axis runs over, the one named last changes fastest.
Arguments:
- inv_interior: bfloat16 [262144, 2048], P('sub'), may hold values from -0.125 to 0.125
- coupling: bfloat16 [262144, 512], P('sub'), may hold values from -0.29882812 to 0.29882812
- boundary: float32 [65536, 512], P('sub'), may hold values from -0.9 to 47
- residual: float32 [65536, 1024], P('sub'), may hold values from -15 to 15
- face_size: int32 [128, 4], P('sub'), may hold values from 64 to 128, as said below
- init_scale: float32 [128, 4], P('sub'), may hold values from 0.008 to 0.016, as said below
Outputs:
- schur: float32 [65536, 512], P('sub')
- averaged: float32 [65536, 1024], P('sub')
- inner: float32 [], replicated
Inputs may be any that keep to these rules, and one draw needn't show every extreme that they name: `face_size`: both sharers of a face give it the same size; some face has 128 unknowns. `init_scale`: both sharers of a face give it the same scaling.
All inputs are finite; a program needn't handle non-finite values.
Results may differ from a plain program's by a relative error of at most 0.0003.
Values sent between devices are 32-bit elements; how exact they have to be, the bound alone decides.
A program may use at most 64 MiB of HBM per device.

v0:
```python
import jax
import jax.numpy as jnp
from jax import lax
from jax.sharding import PartitionSpec as P

FMAX = 128
NS_STEPS = 4


def from_partner(value, axis, stride):
    mask = 2**stride
    pairs = [(source, source ^ mask) for source in range(lax.axis_size(axis))]
    return lax.ppermute(value, axis, pairs)


def face_parts(schur, resid, sizes, faces, width, columns):
    starts = jnp.concatenate([jnp.zeros((1,), jnp.int32), jnp.cumsum(sizes)[:-1]])
    lanes = jnp.arange(width, dtype=jnp.int32)
    valid = (lanes[None, :] < sizes[:, None]).astype(jnp.float32)
    blocks = []
    pieces = []
    for face in range(faces):
        start = starts[face]
        block = lax.dynamic_slice(schur, (start, start), (width, width))
        piece = lax.dynamic_slice(resid, (start, jnp.int32(0)), (width, columns))
        blocks.append(block * valid[face][:, None] * valid[face][None, :])
        pieces.append(piece * valid[face][:, None])
    return (jnp.stack(blocks), jnp.stack(pieces), valid, starts)


def local(inv_interior, coupling, boundary, residual, face_size, init_scale):
    faces = face_size.shape[1]
    width = FMAX
    columns = residual.shape[1]
    high = lax.Precision.HIGHEST
    top_bit = lax.axis_size("sub").bit_length() - 2
    solved = jnp.dot(inv_interior, coupling, preferred_element_type=jnp.float32).astype(
        jnp.bfloat16
    )
    schur = boundary - lax.dot_general(
        coupling, solved, (((0,), (0,)), ((), ())), preferred_element_type=jnp.float32
    )
    blocks, pieces, valid, starts = face_parts(schur, residual, face_size[0], faces, width, columns)
    mate_blocks = []
    mate_rows = []
    for face in range(faces):
        got_block, got_rows = from_partner((blocks[face], pieces[face]), "sub", top_bit - face)
        mate_blocks.append(got_block)
        mate_rows.append(got_rows)
    other_block = jnp.stack(mate_blocks)
    other_rows = jnp.stack(mate_rows)
    total = blocks + other_block
    ident = jnp.eye(width, dtype=jnp.float32)
    approx = init_scale[0][:, None, None] * ident[None] * valid[:, None, :]
    for step in range(NS_STEPS):
        product = jnp.einsum("fij,fjk->fik", total, approx, precision=high)
        approx = 2.0 * approx - jnp.einsum("fij,fjk->fik", approx, product, precision=high)
    weight_own = jnp.einsum("fij,fjk->fik", approx, blocks, precision=high)
    weight_other = jnp.einsum("fij,fjk->fik", approx, other_block, precision=high)
    face_avg = jnp.einsum("fij,fjk->fik", weight_own, pieces, precision=high) + jnp.einsum(
        "fij,fjk->fik", weight_other, other_rows, precision=high
    )
    averaged = residual
    for face in range(faces):
        start = starts[face]
        current = lax.dynamic_slice(averaged, (start, jnp.int32(0)), (width, columns))
        fresh = jnp.where(valid[face][:, None] > 0, face_avg[face], current)
        averaged = lax.dynamic_update_slice(averaged, fresh, (start, jnp.int32(0)))
    inner = lax.psum(jnp.sum(residual * averaged), "sub")
    return (schur, averaged, inner)


def solution(mesh):
    placed = (
        P("sub", None),
        P("sub", None),
        P("sub", None),
        P("sub", None),
        P("sub", None),
        P("sub", None),
    )
    return jax.shard_map(
        local,
        mesh=mesh,
        in_specs=placed,
        out_specs=(P("sub", None), P("sub", None), P()),
        check_vma=False,
    )
```

profile of v0, /device:TPU:1, one launch (start us, length us, event | category | flops | bytes accessed | tf_op | source)
XLA Modules:
  0.0 142.7 jit_solution(16132320076896569465)
XLA Ops:
  0.6 1.0 reduce-window.4
  6.1 0.7 fusion.37
  6.8 2.5 %copy.9 = f32[512,512]{0,1:T(8,128)} copy(f32[512,512]{1,0:T(8,128)} %param.8) | data formatting | bytes 2097152 | tf_op args[2]
  11.3 9.2 %fusion.19 = f32[512,512]{0,1:T(8,128)S(1)} fusion(f32[512,512]{0,1:T(8,128)} %copy.9, bf16[2048,512]{1,0:T(8,128)(2,1)S(1)} %copy-done, bf16[2048,2048]{1,0:T(8,128)(2,1)} %param.6), kind=kOutput, calls=%fused_computation.20 | convolution fusion | flops 5370019840 | bytes 12582912 | tf_op jit(solution)/shard_map/dot_general | solution.py:40
  20.7 4.5 %collective-permute-start = (f32[128,128]{0,1:T(8,128)S(1)}, f32[128,128]{0,1:T(8,128)S(1)}, u32[]{:S(2)}, u32[]{:S(2)}) collective-permute-start(f32[128,128]{0,1:T(8,128)S(1)} %get-tuple-element.10), channel_id=1, source_target_pairs={{0,64},{1,65},{2,66},{3,67},{4,68},{5,69},{6,70},{7,71},{8,72},{9,... | collective-permute-start | bytes 196616 | tf_op jit(solution)/shard_map/ppermute | solution.py:13
  25.2 0.7 collective-permute-start.1
  26.0 2.7 %collective-permute-start.2 = (f32[128,128]{0,1:T(8,128)S(1)}, f32[128,128]{0,1:T(8,128)S(1)}, u32[]{:S(2)}, u32[]{:S(2)}) collective-permute-start(f32[128,128]{0,1:T(8,128)S(1)} %get-tuple-element.12), channel_id=1, source_target_pairs={{0,16},{1,17},{2,18},{3,19},{4,20},{5,21},{6,22},{7,23},{8,24},{9,... | collective-permute-start | bytes 196616 | tf_op jit(solution)/shard_map/ppermute | solution.py:13
  29.0 1.8 %slice_multiply_fusion = (f32[128,1024]{1,0:T(8,128)S(1)}, f32[128,1024]{1,0:T(8,128)S(1)}, f32[128,1024]{1,0:T(8,128)S(1)}, f32[128,1024]{1,0:T(8,128)S(1)}) fusion(f32[512,1024]{1,0:T(8,128)} %param.9, f32[128]{0:T(128)S(1)} %get-tuple-element.18, f32[128]{0:T(128)S(1)} %get-tuple-element.19, s32[]{:T(128)S(6)} %select_n.36, f32[128]{0:T(128)S(1)} %get-tuple-element.20, ...), kind=kLoop, calls=%fused_computation.37 | loop fusion | flops 524288 | bytes 4196364 | tf_op jit(solution)/shard_map/mul | solution.py:27
  30.8 1.0 collective-permute-start.4
  31.9 1.8 %collective-permute-start.6 = (f32[128,1024]{1,0:T(8,128)S(1)}, f32[128,1024]{1,0:T(8,128)S(1)}, u32[]{:S(2)}, u32[]{:S(2)}) collective-permute-start(f32[128,1024]{1,0:T(8,128)S(1)} %get-tuple-element.8), channel_id=1, source_target_pairs={{0,16},{1,17},{2,18},{3,19},{4,20},{5,21},{6,22},{7,23},{8,24},{9,... | collective-permute-start | bytes 1572872 | tf_op jit(solution)/shard_map/ppermute | solution.py:13
  39.3 1.9 %fusion = f32[4,128,1024]{2,1,0:T(8,128)S(1)} fusion(f32[4,128,128]{2,1,0:T(8,128)S(1)} %fusion.28, f32[1,128,1024]{2,1,0:T(8,128)S(1)} %bitcast.81, f32[1,128,1024]{2,1,0:T(8,128)S(1)} %bitcast.82, f32[1,128,1024]{2,1,0:T(8,128)S(1)} %bitcast.83, f32[1,128,1024]{2,1,0:T(8,128)S(1)} %bitcast.84), kind=kOutput, calls=%fused_computation.1 | convolution fusion | flops 806879232 | bytes 4456448 | tf_op jit(solution)/shard_map/fij,fjk->fik/dot_general | solution.py:60
  41.2 2.9 %collective-permute-done.4 = f32[128,1024]{1,0:T(8,128)S(1)} collective-permute-done((f32[128,1024]{1,0:T(8,128)S(1)}, f32[128,1024]{1,0:T(8,128)S(1)}, u32[]{:S(2)}, u32[]{:S(2)}) %collective-permute-start.4) | collective-permute-done | bytes 524320 | tf_op jit(solution)/shard_map/ppermute | solution.py:13
  44.1 9.3 %collective-permute-done.5 = f32[128,1024]{1,0:T(8,128)S(1)} collective-permute-done((f32[128,1024]{1,0:T(8,128)S(1)}, f32[128,1024]{1,0:T(8,128)S(1)}, u32[]{:S(2)}, u32[]{:S(2)}) %collective-permute-start.5) | collective-permute-done | bytes 524320 | tf_op jit(solution)/shard_map/ppermute | solution.py:13
  53.4 1.2 collective-permute-done.7
  54.6 1.9 %fusion.16 = f32[4,128,1024]{2,1,0:T(8,128)S(1)} fusion(f32[4,128,1024]{2,1,0:T(8,128)S(1)} %fusion, f32[4,128,128]{2,1,0:T(8,128)S(1)} %fusion.26, f32[1,128,1024]{2,1,0:T(8,128)S(1)} %bitcast.96, f32[1,128,1024]{2,1,0:T(8,128)S(1)} %bitcast.95, f32[1,128,1024]{2,1,0:T(8,128)S(1)} %bitcast.94, f32[1,128,1024]{2,1,0:T(8,128)S(1)} %bitcast.93), kind=kOutput, calls=%fused_computation.18 | convolution fusion | flops 807403520 | bytes 6553600 | tf_op jit(solution)/shard_map/fij,fjk->fik/dot_general | solution.py:60
  56.7 1.2 copy-done.3
  58.7 2.9 %dynamic_update_slice.13 = f32[512,1024]{1,0:T(8,128)} dynamic-update-slice(f32[512,1024]{1,0:T(8,128)} %copy-done.1, f32[128,1024]{1,0:T(8,128)S(1)} %fusion.22, s32[]{:T(128)S(6)} %select_n.34, s32[]{:T(128)} %constant.2.clone.1) | dynamic-update-slice | bytes 1048580 | tf_op jit(solution)/shard_map/dynamic_update_slice | solution.py:68
  61.7 1.3 fusion.21
  63.0 2.9 %dynamic_update_slice.14 = f32[512,1024]{1,0:T(8,128)} dynamic-update-slice(f32[512,1024]{1,0:T(8,128)} %dynamic_update_slice.13, f32[128,1024]{1,0:T(8,128)S(1)} %fusion.21, s32[]{:T(128)S(6)} %select_n.35, s32[]{:T(128)} %constant.2.clone.1) | dynamic-update-slice | bytes 1048580 | tf_op jit(solution)/shard_map/dynamic_update_slice | solution.py:68
  65.9 1.3 fusion.20
  67.3 2.9 %dynamic_update_slice.15 = f32[512,1024]{1,0:T(8,128)} dynamic-update-slice(f32[512,1024]{1,0:T(8,128)} %dynamic_update_slice.14, f32[128,1024]{1,0:T(8,128)S(1)} %fusion.20, s32[]{:T(128)S(6)} %select_n.36, s32[]{:T(128)} %constant.2.clone.1) | dynamic-update-slice | bytes 1048580 | tf_op jit(solution)/shard_map/dynamic_update_slice | solution.py:68
  70.2 3.5 %multiply_reduce_fusion = f32[]{:T(128)} fusion(f32[512,1024]{1,0:T(8,128)} %param.9, f32[512,1024]{1,0:T(8,128)} %dynamic_update_slice.15), kind=kLoop, calls=%fused_computation.17 | loop fusion | flops 1048575 | bytes 4194308 | tf_op jit(solution)/shard_map/reduce_sum | solution.py:69
  73.7 1.3 copy.10
  75.0 67.8 %psum.7 = f32[]{:T(128)} all-reduce(f32[]{:T(128)} %multiply_reduce_fusion), channel_id=1, replica_groups=mesh['sub'=128] {'sub'}, use_global_device_ids=true, to_apply=%region_2.3 | all-reduce | flops 1 | bytes 8 | tf_op jit(solution)/shard_map/psum | solution.py:69
  (39 shorter events, 7.7 us)
Async XLA Ops:
  0.6 10.7 %copy-start = (bf16[2048,512]{1,0:T(8,128)(2,1)S(1)}, bf16[2048,512]{1,0:T(8,128)(2,1)}, u32[]{:S(2)}) copy-start(bf16[2048,512]{1,0:T(8,128)(2,1)} %param.7) | copy-start | bytes 6291460
  20.5 10.3 %copy-start.4 = (f32[512,512]{0,1:T(8,128)}, f32[512,512]{0,1:T(8,128)S(1)}, u32[]{:S(2)}) copy-start(f32[512,512]{0,1:T(8,128)S(1)} %fusion.19) | copy-start | bytes 3145732
  20.7 11.1 %collective-permute-start = (f32[128,128]{0,1:T(8,128)S(1)}, f32[128,128]{0,1:T(8,128)S(1)}, u32[]{:S(2)}, u32[]{:S(2)}) collective-permute-start(f32[128,128]{0,1:T(8,128)S(1)} %get-tuple-element.10), channel_id=1, source_target_pairs={{0,64},{1,65},{2,66},{3,67},{4,68},{5,69},{6,70},{7,71},{8,72},{9,... | collective-permute-start | bytes 196616 | tf_op jit(solution)/shard_map/ppermute | solution.py:13
  25.2 6.7 %collective-permute-start.1 = (f32[128,128]{0,1:T(8,128)S(1)}, f32[128,128]{0,1:T(8,128)S(1)}, u32[]{:S(2)}, u32[]{:S(2)}) collective-permute-start(f32[128,128]{0,1:T(8,128)S(1)} %get-tuple-element.13), channel_id=1, source_target_pairs={{0,32},{1,33},{2,34},{3,35},{4,36},{5,37},{6,38},{7,39},{8,40},{9,... | collective-permute-start | bytes 196616 | tf_op jit(solution)/shard_map/ppermute | solution.py:13
  26.0 7.8 %collective-permute-start.2 = (f32[128,128]{0,1:T(8,128)S(1)}, f32[128,128]{0,1:T(8,128)S(1)}, u32[]{:S(2)}, u32[]{:S(2)}) collective-permute-start(f32[128,128]{0,1:T(8,128)S(1)} %get-tuple-element.12), channel_id=1, source_target_pairs={{0,16},{1,17},{2,18},{3,19},{4,20},{5,21},{6,22},{7,23},{8,24},{9,... | collective-permute-start | bytes 196616 | tf_op jit(solution)/shard_map/ppermute | solution.py:13
  28.7 5.0 %collective-permute-start.3 = (f32[128,128]{0,1:T(8,128)S(1)}, f32[128,128]{0,1:T(8,128)S(1)}, u32[]{:S(2)}, u32[]{:S(2)}) collective-permute-start(f32[128,128]{0,1:T(8,128)S(1)} %get-tuple-element.11), channel_id=1, source_target_pairs={{0,8},{1,9},{2,10},{3,11},{4,12},{5,13},{6,14},{7,15},{8,0},{9,1},... | collective-permute-start | bytes 196616 | tf_op jit(solution)/shard_map/ppermute | solution.py:13
  30.8 13.3 %collective-permute-start.4 = (f32[128,1024]{1,0:T(8,128)S(1)}, f32[128,1024]{1,0:T(8,128)S(1)}, u32[]{:S(2)}, u32[]{:S(2)}) collective-permute-start(f32[128,1024]{1,0:T(8,128)S(1)} %get-tuple-element.6), channel_id=1, source_target_pairs={{0,64},{1,65},{2,66},{3,67},{4,68},{5,69},{6,70},{7,71},{8,72},{9,... | collective-permute-start | bytes 1572872 | tf_op jit(solution)/shard_map/ppermute | solution.py:13
  31.8 2.0 %copy-start.6 = (f32[1,4]{1,0:T(1,128)S(1)}, f32[1,4]{1,0:T(1,128)}, u32[]{:S(2)}) copy-start(f32[1,4]{1,0:T(1,128)} %param.11) | copy-start | bytes 52
  31.8 21.5 %collective-permute-start.5 = (f32[128,1024]{1,0:T(8,128)S(1)}, f32[128,1024]{1,0:T(8,128)S(1)}, u32[]{:S(2)}, u32[]{:S(2)}) collective-permute-start(f32[128,1024]{1,0:T(8,128)S(1)} %get-tuple-element.9), channel_id=1, source_target_pairs={{0,32},{1,33},{2,34},{3,35},{4,36},{5,37},{6,38},{7,39},{8,40},{9,... | collective-permute-start | bytes 1572872 | tf_op jit(solution)/shard_map/ppermute | solution.py:13
  31.9 21.4 %collective-permute-start.6 = (f32[128,1024]{1,0:T(8,128)S(1)}, f32[128,1024]{1,0:T(8,128)S(1)}, u32[]{:S(2)}, u32[]{:S(2)}) collective-permute-start(f32[128,1024]{1,0:T(8,128)S(1)} %get-tuple-element.8), channel_id=1, source_target_pairs={{0,16},{1,17},{2,18},{3,19},{4,20},{5,21},{6,22},{7,23},{8,24},{9,... | collective-permute-start | bytes 1572872 | tf_op jit(solution)/shard_map/ppermute | solution.py:13
  33.8 20.9 %collective-permute-start.7 = (f32[128,1024]{1,0:T(8,128)S(1)}, f32[128,1024]{1,0:T(8,128)S(1)}, u32[]{:S(2)}, u32[]{:S(2)}) collective-permute-start(f32[128,1024]{1,0:T(8,128)S(1)} %get-tuple-element.7), channel_id=1, source_target_pairs={{0,8},{1,9},{2,10},{3,11},{4,12},{5,13},{6,14},{7,15},{8,0},{9,1},... | collective-permute-start | bytes 1572872 | tf_op jit(solution)/shard_map/ppermute | solution.py:13
  54.6 2.0 %copy-start.2 = (f32[512,1024]{1,0:T(8,128)S(1)}, f32[512,1024]{1,0:T(8,128)}, u32[]{:S(2)}) copy-start(f32[512,1024]{1,0:T(8,128)} %param.9) | copy-start | bytes 6291460
  56.6 1.3 copy-start.3
  56.7 1.8 %copy-start.1 = (f32[512,1024]{1,0:T(8,128)}, f32[512,1024]{1,0:T(8,128)S(1)}, u32[]{:S(2)}) copy-start(f32[512,1024]{1,0:T(8,128)S(1)} %fusion.24) | copy-start | bytes 6291460
  70.2 3.5 %copy-start.5 = (f32[512,512]{0,1:T(8,128)S(1)}, f32[512,512]{0,1:T(8,128)}, u32[]{:S(2)}) copy-start(f32[512,512]{0,1:T(8,128)} %copy-done.4) | copy-start | bytes 3145732
where the time goes:
time: 143 us
  blocking collectives  67.8 us (47%)
  matrix products  18.5 us (13%)
  local copies, waits for them, and re-layouts  15.2 us (11%)
  waiting for transfers between devices  13.4 us (9%)
  starting transfers between devices  11.1 us (8%)
  other arithmetic  10.1 us (7%)
  between operations  6.63 us (5%)
    psum x1, blocking collectives, local(): inner = lax.psum(jnp.sum(residual * averaged), 'sub')  67.8 us
    ppermute x8, waiting for transfers between devices, from_partner(): return lax.ppermute(value, axis, pairs)  13.4 us
    ppermute x8, starting transfers between devices, from_partner(): return lax.ppermute(value, axis, pairs)  11.1 us
    dot_general x1, matrix products, local(): lax.dot_general(coupling, solved, (((0,), (0,)), ((), ())), preferred_ele...  9.21 us
    dynamic_update_slice x3, local copies, waits for them, and re-layouts, local(): averaged = lax.dynamic_update_slice(averaged, fresh, (start, jnp.int32(0)))  8.84 us
    unnamed x16, local copies, waits for them, and re-layouts  5.71 us
    reduce_sum x1, other arithmetic, local(): inner = lax.psum(jnp.sum(residual * averaged), 'sub')  3.45 us
  transfers between devices with their start and end apart: 8, of which 3 were waited for; matrix products, arithmetic and copies ran while one was open for 6% of the time, Pallas kernels for 0%

commit v1 on v0

v1 whole, which is shorter than its diff:
```python
import functools

import jax
import jax.numpy as jnp
from jax import lax
from jax.experimental import pallas as pl
from jax.experimental.pallas import tpu as pltpu
from jax.sharding import PartitionSpec as P

FMAX = 128
STEPS = 4
CHUNKS = 4
EARLY = 2
MROWS = 512
SPAN = FMAX + 8
MESH = pl.DeviceIdType.MESH


def flip(me, mask):
    return me + mask - 2 * mask * ((me // mask) % 2)


def flips(me, masks, which):
    for bit, mask in enumerate(masks):
        if (which >> bit) & 1:
            me = flip(me, mask)
    return me


def rank(me, masks):
    total = 0
    for bit, mask in enumerate(masks):
        total = total + ((me // mask) % 2) * (1 << bit)
    return total


def halves(x):
    hi = x.astype(jnp.bfloat16)
    lo = (x - hi.astype(jnp.float32)).astype(jnp.bfloat16)
    return hi, lo


def mm(a, b):
    return jnp.dot(a, b, preferred_element_type=jnp.float32)


def square_product(a, b):
    ah, al = halves(a)
    bh, bl = halves(b)
    row = jnp.concatenate([bh, bl], axis=1)
    both = mm(jnp.concatenate([ah, al], axis=1), jnp.concatenate([row, row], axis=0))
    return both[:, :FMAX] + both[:, FMAX:]


def turned(x, shift):
    amount = jnp.full((1, 8, x.shape[2]), shift, jnp.int32)
    for bit in (1, 2, 4):
        x = jnp.where((amount & bit) != 0, jnp.roll(x, bit, axis=1), x)
    return x


def rows_at(ref, start, columns):
    base = jnp.minimum(lax.div(start, 8), (ref.shape[0] - FMAX) // 8 - 1) * 8
    shift = start - base
    x = ref[pl.ds(base, FMAX + 8), columns]
    w = x.shape[1]
    x = turned(x.reshape(FMAX // 8 + 1, 8, w), 8 - shift)
    row = lax.broadcasted_iota(jnp.int32, (1, 8, w), 1)
    return jnp.where(row < 8 - shift, x[:-1], x[1:]).reshape(FMAX, w)


def rows_down(x, shift):
    w = x.shape[1]
    pad = jnp.zeros((1, 8, w), x.dtype)
    x = jnp.concatenate([pad, x.reshape(FMAX // 8, 8, w), pad], axis=0)
    x = turned(x, shift)
    row = lax.broadcasted_iota(jnp.int32, (1, 8, w), 1)
    return jnp.where(row < shift, x[:-1], x[1:]).reshape(FMAX + 8, w)


def kernel(
    masks,
    groups,
    inv_hbm,
    cpl_hbm,
    bnd_hbm,
    res_hbm,
    size_ref,
    scale_ref,
    schur_ref,
    avg_ref,
    inner_ref,
    inv,
    cpl,
    sol,
    bnd,
    res,
    own,
    oth,
    own_b,
    oth_b,
    face,
    wbuf,
    red,
    in_sem,
    inv_sem,
    s_sem,
    r_sem,
    sb_sem,
    rb_sem,
    sr_sem,
    rr_sem,
):
    me = lax.axis_index("sub")
    faces = len(masks)
    ni, nb = cpl.shape
    columns = res.shape[1]
    width = columns // CHUNKS

    load_res = pltpu.make_async_copy(res_hbm, res, in_sem.at[0])
    load_res.start()
    load_cpl = pltpu.make_async_copy(cpl_hbm, cpl, in_sem.at[1])
    load_cpl.start()
    load_inv = [
        pltpu.make_async_copy(
            inv_hbm.at[pl.ds(i * MROWS, MROWS)], inv.at[pl.ds(i * MROWS, MROWS)], inv_sem.at[i]
        )
        for i in range(ni // MROWS)
    ]
    for copy in load_inv:
        copy.start()
    load_bnd = pltpu.make_async_copy(bnd_hbm, bnd, in_sem.at[2])
    load_bnd.start()

    mates = [flip(me, mask) for mask in masks]
    peers = []
    for group in groups:
        peers += [flips(me, group, which) for which in range(1, 1 << len(group))]
    barrier = pltpu.get_barrier_semaphore()
    for peer in peers:
        pl.semaphore_signal(barrier, inc=1, device_id=(peer,), device_id_type=MESH)

    odd = 0
    for mask in masks:
        odd = odd + (me // mask) % 2
    odd = odd % 2
    sizes = [size_ref[0, r] for r in range(faces)]
    starts = [jnp.int32(0)]
    for r in range(faces):
        starts.append(starts[-1] + sizes[r])
    whole = [lax.div(start, 8) * 8 for start in starts]
    face[...] = jnp.zeros_like(face)

    load_res.wait()
    rows = lax.broadcasted_iota(jnp.int32, (FMAX, width), 0)
    for k in range(CHUNKS):
        c = (1 - odd) * k + odd * (CHUNKS - 1 - k)
        at = pl.multiple_of(c * width, width)
        for r in range(faces):
            piece = rows_at(res, starts[r], pl.ds(at, width))
            own[k, r] = jnp.where(rows < sizes[r], piece, 0.0)

    pl.semaphore_wait(barrier, len(peers))
    copies = [
        [
            pltpu.make_async_remote_copy(
                src_ref=own.at[k, r],
                dst_ref=oth.at[k, r],
                send_sem=s_sem.at[k, r],
                recv_sem=r_sem.at[k, r],
                device_id=(mates[r],),
                device_id_type=MESH,
            )
            for r in range(faces)
        ]
        for k in range(CHUNKS)
    ]
    for k in range(EARLY):
        for r in range(faces):
            copies[k][r].start()

    load_cpl.wait()
    for i in range(ni // MROWS):
        load_inv[i].wait()
        sol[pl.ds(i * MROWS, MROWS), :] = mm(inv[pl.ds(i * MROWS, MROWS), :], cpl[...]).astype(
            jnp.bfloat16
        )
    load_bnd.wait()
    schur_ref[...] = bnd[...] - lax.dot_general(
        cpl[...], sol[...], (((0,), (0,)), ((), ())), preferred_element_type=jnp.float32
    )

    i0 = lax.broadcasted_iota(jnp.int32, (FMAX, FMAX), 0)
    i1 = lax.broadcasted_iota(jnp.int32, (FMAX, FMAX), 1)
    for r in range(faces):
        left = jnp.minimum(lax.div(starts[r], FMAX), nb // FMAX - 2) * FMAX
        band = rows_at(schur_ref, starts[r], pl.ds(left, 2 * FMAX))
        b0 = lax.broadcasted_iota(jnp.int32, (2 * FMAX, FMAX), 0)
        b1 = lax.broadcasted_iota(jnp.int32, (2 * FMAX, FMAX), 1)
        pick = jnp.where(b0 == b1 + (starts[r] - left), 1.0, 0.0).astype(jnp.bfloat16)
        hi, lo = halves(band)
        rest = band - hi.astype(jnp.float32) - lo.astype(jnp.float32)
        parts = mm(jnp.concatenate([hi, lo, rest.astype(jnp.bfloat16)], axis=0), pick)
        block = parts[:FMAX] + parts[FMAX : 2 * FMAX] + parts[2 * FMAX :]
        own_b[r] = jnp.where((i0 < sizes[r]) & (i1 < sizes[r]), block, 0.0)
    block_copies = [
        pltpu.make_async_remote_copy(
            src_ref=own_b.at[r],
            dst_ref=oth_b.at[r],
            send_sem=sb_sem.at[r],
            recv_sem=rb_sem.at[r],
            device_id=(mates[r],),
            device_id_type=MESH,
        )
        for r in range(faces)
    ]
    for copy in block_copies:
        copy.start()
    for k in range(EARLY, CHUNKS):
        for r in range(faces):
            copies[k][r].start()

    es, xs = [], []
    for r in range(faces):
        block_copies[r].wait_recv()
        scale = scale_ref[0, r]
        ident = jnp.where((i0 == i1) & (i0 < sizes[r]), 1.0, 0.0)
        e = ident - scale * (own_b[r] + oth_b[r])
        xs.append(scale * (ident + e))
        es.append(e)
    for step in range(1, STEPS):
        es = [square_product(e, e) for e in es]
        xs = [x + square_product(x, e) for x, e in zip(xs, es)]
    for r in range(faces):
        w = jnp.concatenate(
            [square_product(xs[r], own_b[r]), square_product(xs[r], oth_b[r])], axis=1
        )
        wh, wl = halves(w)
        wbuf[r, pl.ds(0, FMAX), :] = wh
        wbuf[r, pl.ds(FMAX, FMAX), :] = wl

    def fold(x):
        total = None
        for a in range(0, x.shape[0], 8):
            for b in range(0, x.shape[1], 128):
                t = x[a : a + 8, b : b + 128]
                total = t if total is None else total + t
        return total

    row8 = lax.broadcasted_iota(jnp.int32, (8, 128), 0)
    partial = jnp.zeros((8, 128), jnp.float32)
    low = faces * (FMAX // 2)
    for a in range(low, nb, 8):
        t = res[pl.ds(a, 8), :]
        t = fold(t * t)
        partial = partial + jnp.where(row8 + a >= starts[faces], t, 0.0)

    for k in range(CHUNKS):
        c = odd * k + (1 - odd) * (CHUNKS - 1 - k)
        at = pl.multiple_of(c * width, width)
        for r in range(faces):
            copies[k][r].wait_recv()
            mine, theirs = own[CHUNKS - 1 - k, r], oth[k, r]
            ph, pw = halves(jnp.concatenate([mine, theirs], axis=0))
            top = mm(wbuf[r], ph)
            value = top[:FMAX] + top[FMAX:] + mm(wbuf[r, pl.ds(0, FMAX), :], pw)
            face[pl.ds(r * SPAN, SPAN), :] = rows_down(value, starts[r] - whole[r])
            if k < CHUNKS // 2:
                partial = partial + fold((mine + theirs) * value)
        for a in range(0, nb, 8):
            t = res[pl.ds(a, 8), pl.ds(at, width)]
            here = lax.broadcasted_iota(jnp.int32, (8, width), 0) + a
            for r in range(faces):
                if a >= r * (FMAX // 2) and a < (r + 1) * FMAX:
                    tile = a // 8 + r * (SPAN // 8) - lax.div(starts[r], 8)
                    tile = jnp.clip(tile, 0, face.shape[0] // 8 - 1)
                    shifted = face[pl.ds(tile * 8, 8), :]
                    t = jnp.where((here >= starts[r]) & (here < starts[r + 1]), shifted, t)
            avg_ref[pl.ds(a, 8), pl.ds(at, width)] = t

    base = 0
    sends = []
    for g, group in enumerate(groups):
        mine = rank(me, group)
        red[base + mine] = partial
        n = 1 << len(group)
        round_copies = []
        for which in range(1, n):
            round_copies.append(
                pltpu.make_async_remote_copy(
                    src_ref=red.at[base + mine],
                    dst_ref=red.at[base + mine],
                    send_sem=sr_sem.at[base + which],
                    recv_sem=rr_sem.at[base + which],
                    device_id=(flips(me, group, which),),
                    device_id_type=MESH,
                )
            )
        for copy in round_copies:
            copy.start()
        for copy in round_copies:
            copy.wait_recv()
        sends += round_copies
        partial = red[base]
        for j in range(1, n):
            partial = partial + red[base + j]
        base += n
    inner_ref[0, 0] = jnp.sum(partial)

    for copy in sends:
        copy.wait_send()
    for copy in block_copies:
        copy.wait_send()
    for row in copies:
        for copy in row:
            copy.wait_send()


def local(inv_interior, coupling, boundary, residual, face_size, init_scale):
    ni, nb = coupling.shape
    columns = residual.shape[1]
    faces = face_size.shape[1]
    subs = lax.axis_size("sub")
    masks = [subs >> (r + 1) for r in range(faces)]
    groups = [[1, 2, 4], [8, 16], [32, 64]]
    slots = sum(1 << len(g) for g in groups)
    width = columns // CHUNKS
    f32, bf16 = jnp.float32, jnp.bfloat16
    anyspec = pl.BlockSpec(memory_space=pl.ANY)
    smem = pl.BlockSpec(memory_space=pltpu.SMEM)
    vmem = pl.BlockSpec(memory_space=pltpu.VMEM)
    dma = pltpu.SemaphoreType.DMA
    schur, averaged, inner = pl.pallas_call(
        functools.partial(kernel, masks, groups),
        name="deluxe",
        out_shape=(
            jax.ShapeDtypeStruct((nb, nb), f32),
            jax.ShapeDtypeStruct((nb, columns), f32),
            jax.ShapeDtypeStruct((1, 1), f32),
        ),
        in_specs=[anyspec, anyspec, anyspec, anyspec, smem, smem],
        out_specs=(vmem, vmem, smem),
        scratch_shapes=[
            pltpu.VMEM((ni, ni), bf16),
            pltpu.VMEM((ni, nb), bf16),
            pltpu.VMEM((ni, nb), bf16),
            pltpu.VMEM((nb, nb), f32),
            pltpu.VMEM((nb, columns), f32),
            pltpu.VMEM((CHUNKS, faces, FMAX, width), f32),
            pltpu.VMEM((CHUNKS, faces, FMAX, width), f32),
            pltpu.VMEM((faces, FMAX, FMAX), f32),
            pltpu.VMEM((faces, FMAX, FMAX), f32),
            pltpu.VMEM((faces * SPAN + (faces - 1) * (FMAX // 2) - 8, width), f32),
            pltpu.VMEM((faces, 2 * FMAX, 2 * FMAX), bf16),
            pltpu.VMEM((slots, 8, 128), f32),
            dma((3,)),
            dma((ni // MROWS,)),
            dma((CHUNKS, faces)),
            dma((CHUNKS, faces)),
            dma((faces,)),
            dma((faces,)),
            dma((slots,)),
            dma((slots,)),
        ],
        compiler_params=pltpu.CompilerParams(
            collective_id=0, has_side_effects=True, vmem_limit_bytes=56 * 2**20
        ),
    )(inv_interior, coupling, boundary, residual, face_size, init_scale)
    return (schur, averaged, inner[0, 0])


def solution(mesh):
    spec = P("sub", None)
    return jax.shard_map(
        local,
        mesh=mesh,
        in_specs=(spec,) * 6,
        out_specs=(spec, spec, P()),
        check_vma=False,
    )
```

time: 143 us -> 56 us (0.39)
  blocking collectives: 67.8 us -> 0 us
  Pallas kernels: 0 us -> 48.9 us
  matrix products: 18.5 us -> 0 us
  waiting for transfers between devices: 13.4 us -> 0 us
  local copies, waits for them, and re-layouts: 15.2 us -> 3.73 us
  starting transfers between devices: 11.1 us -> 0 us
  other arithmetic: 10.1 us -> 0 us
  between operations: 6.63 us -> 2.47 us
    psum x1 -> x0, blocking collectives: 67.8 us -> none  [local(): inner = lax.psum(jnp.sum(residual * averaged), 'sub')]
    pallas_call x0 -> x1, Pallas kernels: none -> 48.9 us  [local(): pl.pallas_call(functools.partial(kernel, masks, groups), name='deluxe', o...]
    dot_general x13 -> x0, matrix products: 18.5 us -> none  [the longest x1 9.21 us: local(): lax.dot_general(coupling, solved, (((0,), (0,)), ((), ())), preferred_ele...]
    ppermute x8 -> x0, waiting for transfers between devices: 13.4 us -> none  [from_partner(): return lax.ppermute(value, axis, pairs)]
    ppermute x8 -> x0, starting transfers between devices: 11.1 us -> none  [from_partner(): return lax.ppermute(value, axis, pairs)]
    dynamic_update_slice x3 -> x0, local copies, waits for them, and re-layouts: 8.84 us -> none  [local(): averaged = lax.dynamic_update_slice(averaged, fresh, (start, jnp.int32(0)))]
    reduce_sum x1 -> x0, other arithmetic: 3.45 us -> none  [local(): inner = lax.psum(jnp.sum(residual * averaged), 'sub')]
    select_n x3 -> x0, other arithmetic: 2.77 us -> none  [local(): fresh = jnp.where(valid[face][:, None] > 0, face_avg[face], current)]
  transfers between devices with their start and end apart: 8 -> 0, of which waited for: 3 -> 0; matrix products, arithmetic and copies ran while one was open for 6% -> 0% of each run, Pallas kernels for 0% -> 0%
where the time goes in v1:
time: 56 us; the launch traced here: 55.1 us
  Pallas kernels  48.9 us (87%)
  local copies, waits for them, and re-layouts  3.73 us (7%)
  between operations  2.47 us (4%)
    pallas_call x1, Pallas kernels, local(): pl.pallas_call(functools.partial(kernel, masks, groups), name='deluxe', o...  48.9 us
    unnamed x4, local copies, waits for them, and re-layouts  3.73 us

profile of v1, /device:TPU:1, one launch (start us, length us, event | category | flops | bytes accessed | tf_op | source)
XLA Modules:
  0.0 55.1 jit_solution(16446105522217067571)
XLA Ops:
  0.6 48.9 %deluxe.1 = (f32[512,512]{1,0:T(8,128)}, f32[512,1024]{1,0:T(8,128)}, f32[1,1]{1,0:T(1,128)}) custom-call(bf16[2048,2048]{1,0:T(8,128)(2,1)} %inv_hbm.1, bf16[2048,512]{1,0:T(8,128)(2,1)} %cpl_hbm.1, f32[512,512]{1,0:T(8,128)} %bnd_hbm.1, f32[512,1024]{1,0:T(8,128)} %res_hbm.1, s32[1,4]{1,0:T(1,128)} %size_ref.1, f32[1,4]{1,0:T(1,128)} %scale_ref.1), custom_call_target="tpu_custom_call" | custom-call | tf_op jit(solution)/shard_map/deluxe/pallas_call | solution.py:333
  49.5 0.0 copy-start
  49.5 2.4 %copy.12 = f32[512,512]{1,0:T(8,128)} copy(f32[512,512]{1,0:T(8,128)} %get-tuple-element.12) | data formatting | bytes 2097152
  51.9 0.0 copy-done
  51.9 1.3 %copy.13 = f32[512,1024]{1,0:T(8,128)} copy(f32[512,1024]{1,0:T(8,128)S(1)} %copy-done) | data formatting | bytes 4194304
Async XLA Ops:
  49.5 2.4 %copy-start = (f32[512,1024]{1,0:T(8,128)S(1)}, f32[512,1024]{1,0:T(8,128)}, u32[]{:S(2)}) copy-start(f32[512,1024]{1,0:T(8,128)} %get-tuple-element.13) | copy-start | bytes 6291460

commit v2 on v1

--- a/solution.py
+++ b/solution.py
@@ -9,8 +9,9 @@
 
 FMAX = 128
 STEPS = 4
-CHUNKS = 4
-EARLY = 2
+CHUNKS = 8
+EARLY = 3
+HALF = CHUNKS // 2
 MROWS = 512
 SPAN = FMAX + 8
 MESH = pl.DeviceIdType.MESH
@@ -119,6 +120,26 @@
 
     load_res = pltpu.make_async_copy(res_hbm, res, in_sem.at[0])
     load_res.start()
+    mates = [flip(me, mask) for mask in masks]
+    peers = []
+    for group in groups:
+        peers += [flips(me, group, which) for which in range(1, 1 << len(group))]
+    barrier = pltpu.get_barrier_semaphore()
+    for peer in peers:
+        pl.semaphore_signal(barrier, inc=1, device_id=(peer,), device_id_type=MESH)
+
+    odd = 0
+    for mask in masks:
+        odd = odd + (me // mask) % 2
+    odd = odd % 2
+    sizes = [size_ref[0, r] for r in range(faces)]
+    starts = [jnp.int32(0)]
+    for r in range(faces):
+        starts.append(starts[-1] + sizes[r])
+    whole = [lax.div(start, 8) * 8 for start in starts]
+    face[...] = jnp.zeros_like(face)
+
+    load_res.wait()
     load_cpl = pltpu.make_async_copy(cpl_hbm, cpl, in_sem.at[1])
     load_cpl.start()
     load_inv = [
@@ -132,35 +153,6 @@
     load_bnd = pltpu.make_async_copy(bnd_hbm, bnd, in_sem.at[2])
     load_bnd.start()
 
-    mates = [flip(me, mask) for mask in masks]
-    peers = []
-    for group in groups:
-        peers += [flips(me, group, which) for which in range(1, 1 << len(group))]
-    barrier = pltpu.get_barrier_semaphore()
-    for peer in peers:
-        pl.semaphore_signal(barrier, inc=1, device_id=(peer,), device_id_type=MESH)
-
-    odd = 0
-    for mask in masks:
-        odd = odd + (me // mask) % 2
-    odd = odd % 2
-    sizes = [size_ref[0, r] for r in range(faces)]
-    starts = [jnp.int32(0)]
-    for r in range(faces):
-        starts.append(starts[-1] + sizes[r])
-    whole = [lax.div(start, 8) * 8 for start in starts]
-    face[...] = jnp.zeros_like(face)
-
-    load_res.wait()
-    rows = lax.broadcasted_iota(jnp.int32, (FMAX, width), 0)
-    for k in range(CHUNKS):
-        c = (1 - odd) * k + odd * (CHUNKS - 1 - k)
-        at = pl.multiple_of(c * width, width)
-        for r in range(faces):
-            piece = rows_at(res, starts[r], pl.ds(at, width))
-            own[k, r] = jnp.where(rows < sizes[r], piece, 0.0)
-
-    pl.semaphore_wait(barrier, len(peers))
     copies = [
         [
             pltpu.make_async_remote_copy(
@@ -175,9 +167,22 @@
         ]
         for k in range(CHUNKS)
     ]
-    for k in range(EARLY):
+
+    def issue(k):
         for r in range(faces):
             copies[k][r].start()
+
+    rows = lax.broadcasted_iota(jnp.int32, (FMAX, width), 0)
+    for k in range(CHUNKS):
+        c = (1 - odd) * k + odd * (CHUNKS - 1 - k)
+        at = pl.multiple_of(c * width, width)
+        for r in range(faces):
+            piece = rows_at(res, starts[r], pl.ds(at, width))
+            own[k, r] = jnp.where(rows < sizes[r], piece, 0.0)
+        if k == 1:
+            pl.semaphore_wait(barrier, len(peers))
+        if 1 <= k <= EARLY:
+            issue(k - 1)
 
     load_cpl.wait()
     for i in range(ni // MROWS):
@@ -216,9 +221,8 @@
     ]
     for copy in block_copies:
         copy.start()
-    for k in range(EARLY, CHUNKS):
-        for r in range(faces):
-            copies[k][r].start()
+    for k in range(EARLY, HALF + 2):
+        issue(k)
 
     es, xs = [], []
     for r in range(faces):
@@ -255,56 +259,83 @@
         t = fold(t * t)
         partial = partial + jnp.where(row8 + a >= starts[faces], t, 0.0)
 
-    for k in range(CHUNKS):
-        c = odd * k + (1 - odd) * (CHUNKS - 1 - k)
-        at = pl.multiple_of(c * width, width)
+    def finish(ks):
+        pair = jnp.zeros((8, 128), jnp.float32)
+        values = []
         for r in range(faces):
-            copies[k][r].wait_recv()
-            mine, theirs = own[CHUNKS - 1 - k, r], oth[k, r]
-            ph, pw = halves(jnp.concatenate([mine, theirs], axis=0))
+            for k in ks:
+                copies[k][r].wait_recv()
+            both = [jnp.concatenate([own[CHUNKS - 1 - k, r], oth[k, r]], axis=0) for k in ks]
+            ph, pw = halves(jnp.concatenate(both, axis=1))
             top = mm(wbuf[r], ph)
             value = top[:FMAX] + top[FMAX:] + mm(wbuf[r, pl.ds(0, FMAX), :], pw)
-            face[pl.ds(r * SPAN, SPAN), :] = rows_down(value, starts[r] - whole[r])
-            if k < CHUNKS // 2:
-                partial = partial + fold((mine + theirs) * value)
-        for a in range(0, nb, 8):
-            t = res[pl.ds(a, 8), pl.ds(at, width)]
-            here = lax.broadcasted_iota(jnp.int32, (8, width), 0) + a
+            values.append(value)
+            for j, k in enumerate(ks):
+                if k < HALF:
+                    part = value[:, j * width : (j + 1) * width]
+                    pair = pair + fold((both[j][:FMAX] + both[j][FMAX:]) * part)
+        for j, k in enumerate(ks):
+            c = odd * k + (1 - odd) * (CHUNKS - 1 - k)
+            at = pl.multiple_of(c * width, width)
             for r in range(faces):
-                if a >= r * (FMAX // 2) and a < (r + 1) * FMAX:
-                    tile = a // 8 + r * (SPAN // 8) - lax.div(starts[r], 8)
-                    tile = jnp.clip(tile, 0, face.shape[0] // 8 - 1)
-                    shifted = face[pl.ds(tile * 8, 8), :]
-                    t = jnp.where((here >= starts[r]) & (here < starts[r + 1]), shifted, t)
-            avg_ref[pl.ds(a, 8), pl.ds(at, width)] = t
-
-    base = 0
-    sends = []
-    for g, group in enumerate(groups):
-        mine = rank(me, group)
-        red[base + mine] = partial
-        n = 1 << len(group)
-        round_copies = []
-        for which in range(1, n):
-            round_copies.append(
-                pltpu.make_async_remote_copy(
-                    src_ref=red.at[base + mine],
-                    dst_ref=red.at[base + mine],
-                    send_sem=sr_sem.at[base + which],
-                    recv_sem=rr_sem.at[base + which],
-                    device_id=(flips(me, group, which),),
-                    device_id_type=MESH,
-                )
+                part = values[r][:, j * width : (j + 1) * width]
+                face[k % 2, pl.ds(r * SPAN, SPAN), :] = rows_down(part, starts[r] - whole[r])
+            here = lax.broadcasted_iota(jnp.int32, (8, width), 0)
+            for a in range(0, nb, 8):
+                t = res[pl.ds(a, 8), pl.ds(at, width)]
+                for r in range(faces):
+                    if a >= r * (FMAX // 2) and a < (r + 1) * FMAX:
+                        tile = a // 8 + r * (SPAN // 8) - lax.div(starts[r], 8)
+                        tile = jnp.clip(tile, 0, face.shape[1] // 8 - 1)
+                        shifted = face[k % 2, pl.ds(tile * 8, 8), :]
+                        t = jnp.where(
+                            (here >= starts[r] - a) & (here < starts[r + 1] - a), shifted, t
+                        )
+                avg_ref[pl.ds(a, 8), pl.ds(at, width)] = t
+        return pair
+
+    bases = [0]
+    for group in groups:
+        bases.append(bases[-1] + (1 << len(group)))
+
+    def spread(g, value):
+        mine = bases[g] + rank(me, groups[g])
+        red[mine] = value
+        round_copies = [
+            pltpu.make_async_remote_copy(
+                src_ref=red.at[mine],
+                dst_ref=red.at[mine],
+                send_sem=sr_sem.at[bases[g] + which],
+                recv_sem=rr_sem.at[bases[g] + which],
+                device_id=(flips(me, groups[g], which),),
+                device_id_type=MESH,
             )
+            for which in range(1, 1 << len(groups[g]))
+        ]
         for copy in round_copies:
             copy.start()
+        return round_copies
+
+    def gather(g, round_copies):
         for copy in round_copies:
             copy.wait_recv()
+        total = red[bases[g]]
+        for j in range(bases[g] + 1, bases[g + 1]):
+            total = total + red[j]
+        return total
+
+    for k in range(0, HALF, 2):
+        partial = partial + finish((k, k + 1))
+    sends = []
+    for g in range(len(groups)):
+        round_copies = spread(g, partial)
         sends += round_copies
-        partial = red[base]
-        for j in range(1, n):
-            partial = partial + red[base + j]
-        base += n
+        if HALF + 2 + g < CHUNKS:
+            issue(HALF + 2 + g)
+        finish((HALF + g,))
+        partial = gather(g, round_copies)
+    for k in range(HALF + len(groups), CHUNKS):
+        finish((k,))
     inner_ref[0, 0] = jnp.sum(partial)
 
     for copy in sends:
@@ -322,7 +353,7 @@
     faces = face_size.shape[1]
     subs = lax.axis_size("sub")
     masks = [subs >> (r + 1) for r in range(faces)]
-    groups = [[1, 2, 4], [8, 16], [32, 64]]
+    groups = [[8, 16], [32, 64], [1, 2, 4]]
     slots = sum(1 << len(g) for g in groups)
     width = columns // CHUNKS
     f32, bf16 = jnp.float32, jnp.bfloat16
@@ -334,8 +365,8 @@
         functools.partial(kernel, masks, groups),
         name="deluxe",
         out_shape=(
-            jax.ShapeDtypeStruct((nb, nb), f32),
-            jax.ShapeDtypeStruct((nb, columns), f32),
+            pltpu.VMEM((nb, nb), f32),
+            pltpu.VMEM((nb, columns), f32),
             jax.ShapeDtypeStruct((1, 1), f32),
         ),
         in_specs=[anyspec, anyspec, anyspec, anyspec, smem, smem],
@@ -350,7 +381,7 @@
             pltpu.VMEM((CHUNKS, faces, FMAX, width), f32),
             pltpu.VMEM((faces, FMAX, FMAX), f32),
             pltpu.VMEM((faces, FMAX, FMAX), f32),
-            pltpu.VMEM((faces * SPAN + (faces - 1) * (FMAX // 2) - 8, width), f32),
+            pltpu.VMEM((2, faces * SPAN + (faces - 1) * (FMAX // 2) - 8, width), f32),
             pltpu.VMEM((faces, 2 * FMAX, 2 * FMAX), bf16),
             pltpu.VMEM((slots, 8, 128), f32),
             dma((3,)),

time: 56 us -> 47.2 us (0.84); the launches traced: 55.1 us -> 47 us
  Pallas kernels: 48.9 us -> 42.4 us
  local copies, waits for them, and re-layouts: 3.73 us -> 2.29 us
    pallas_call x1, Pallas kernels: 48.9 us -> 42.4 us  [local(): pl.pallas_call(functools.partial(kernel, masks, groups), name='deluxe', o...]
    unnamed x4 -> x2, local copies, waits for them, and re-layouts: 3.73 us -> 2.29 us
where the time goes in v2:
time: 47.2 us; the launch traced here: 47 us
  Pallas kernels  42.4 us (90%)
  between operations  2.33 us (5%)
  local copies, waits for them, and re-layouts  2.29 us (5%)
    pallas_call x1, Pallas kernels, local(): pl.pallas_call(functools.partial(kernel, masks, groups), name='deluxe', o...  42.4 us
    unnamed x2, local copies, waits for them, and re-layouts  2.29 us

profile of v2, /device:TPU:1, one launch (start us, length us, event | category | flops | bytes accessed | tf_op | source)
XLA Modules:
  0.0 47.0 jit_solution(4856825203994735786)
XLA Ops:
  0.6 42.4 %deluxe.1 = (f32[512,512]{1,0:T(8,128)S(1)}, f32[512,1024]{1,0:T(8,128)S(1)}, f32[1,1]{1,0:T(1,128)}) custom-call(bf16[2048,2048]{1,0:T(8,128)(2,1)} %inv_hbm.1, bf16[2048,512]{1,0:T(8,128)(2,1)} %cpl_hbm.1, f32[512,512]{1,0:T(8,128)} %bnd_hbm.1, f32[512,1024]{1,0:T(8,128)} %res_hbm.1, s32[1,4]{1,0:T(1,128)} %size_ref.1, f32[1,4]{1,0:T(1,128)} %scale_ref.1), custom_call_target="tpu_custom_call" | custom-call | tf_op jit(solution)/shard_map/deluxe/pallas_call | solution.py:364
  43.0 1.0 %copy.12 = f32[512,512]{1,0:T(8,128)} copy(f32[512,512]{1,0:T(8,128)S(1)} %get-tuple-element.9) | data formatting | bytes 2097152
  44.0 1.3 %copy.13 = f32[512,1024]{1,0:T(8,128)} copy(f32[512,1024]{1,0:T(8,128)S(1)} %get-tuple-element.10) | data formatting | bytes 4194304

commit v3 on v2

--- a/solution.py
+++ b/solution.py
@@ -173,23 +173,31 @@
             copies[k][r].start()
 
     rows = lax.broadcasted_iota(jnp.int32, (FMAX, width), 0)
-    for k in range(CHUNKS):
+
+    def extract(k):
         c = (1 - odd) * k + odd * (CHUNKS - 1 - k)
         at = pl.multiple_of(c * width, width)
         for r in range(faces):
             piece = rows_at(res, starts[r], pl.ds(at, width))
             own[k, r] = jnp.where(rows < sizes[r], piece, 0.0)
-        if k == 1:
-            pl.semaphore_wait(barrier, len(peers))
-        if 1 <= k <= EARLY:
-            issue(k - 1)
-
+
+    extract(0)
+    extract(1)
+    pl.semaphore_wait(barrier, len(peers))
+    issue(0)
     load_cpl.wait()
-    for i in range(ni // MROWS):
+    steps = ni // MROWS
+    for i in range(steps):
         load_inv[i].wait()
+        if i + 2 < CHUNKS:
+            extract(i + 2)
         sol[pl.ds(i * MROWS, MROWS), :] = mm(inv[pl.ds(i * MROWS, MROWS), :], cpl[...]).astype(
             jnp.bfloat16
         )
+        if i + 1 < EARLY:
+            issue(i + 1)
+    for k in range(steps + 2, CHUNKS):
+        extract(k)
     load_bnd.wait()
     schur_ref[...] = bnd[...] - lax.dot_general(
         cpl[...], sol[...], (((0,), (0,)), ((), ())), preferred_element_type=jnp.float32
@@ -326,6 +334,7 @@
 
     for k in range(0, HALF, 2):
         partial = partial + finish((k, k + 1))
+    partial = jnp.sum(partial, axis=0, keepdims=True)
     sends = []
     for g in range(len(groups)):
         round_copies = spread(g, partial)
@@ -347,13 +356,25 @@
             copy.wait_send()
 
 
+def copy_out(schur_ref, avg_ref, inner_ref, schur_out, avg_out, inner_out, sem):
+    copies = [
+        pltpu.make_async_copy(avg_ref, avg_out, sem.at[0]),
+        pltpu.make_async_copy(schur_ref, schur_out, sem.at[1]),
+    ]
+    for copy in copies:
+        copy.start()
+    inner_out[0, 0] = inner_ref[0, 0]
+    for copy in copies:
+        copy.wait()
+
+
 def local(inv_interior, coupling, boundary, residual, face_size, init_scale):
     ni, nb = coupling.shape
     columns = residual.shape[1]
     faces = face_size.shape[1]
     subs = lax.axis_size("sub")
     masks = [subs >> (r + 1) for r in range(faces)]
-    groups = [[8, 16], [32, 64], [1, 2, 4]]
+    groups = [[1, 2, 4], [8, 16, 32, 64]]
     slots = sum(1 << len(g) for g in groups)
     width = columns // CHUNKS
     f32, bf16 = jnp.float32, jnp.bfloat16
@@ -367,7 +388,7 @@
         out_shape=(
             pltpu.VMEM((nb, nb), f32),
             pltpu.VMEM((nb, columns), f32),
-            jax.ShapeDtypeStruct((1, 1), f32),
+            pltpu.SMEM((1, 1), f32),
         ),
         in_specs=[anyspec, anyspec, anyspec, anyspec, smem, smem],
         out_specs=(vmem, vmem, smem),
@@ -383,7 +404,7 @@
             pltpu.VMEM((faces, FMAX, FMAX), f32),
             pltpu.VMEM((2, faces * SPAN + (faces - 1) * (FMAX // 2) - 8, width), f32),
             pltpu.VMEM((faces, 2 * FMAX, 2 * FMAX), bf16),
-            pltpu.VMEM((slots, 8, 128), f32),
+            pltpu.VMEM((slots, 1, 128), f32),
             dma((3,)),
             dma((ni // MROWS,)),
             dma((CHUNKS, faces)),
@@ -397,6 +418,22 @@
             collective_id=0, has_side_effects=True, vmem_limit_bytes=56 * 2**20
         ),
     )(inv_interior, coupling, boundary, residual, face_size, init_scale)
+    schur, averaged, inner = pl.pallas_call(
+        copy_out,
+        name="copy_out",
+        out_shape=(
+            jax.ShapeDtypeStruct((nb, nb), f32),
+            jax.ShapeDtypeStruct((nb, columns), f32),
+            jax.ShapeDtypeStruct((1, 1), f32),
+        ),
+        in_specs=[vmem, vmem, smem],
+        out_specs=(anyspec, anyspec, smem),
+        scratch_shapes=[dma((2,))],
+    )(
+        pltpu.with_memory_space_constraint(schur, pltpu.VMEM),
+        pltpu.with_memory_space_constraint(averaged, pltpu.VMEM),
+        pltpu.with_memory_space_constraint(inner, pltpu.SMEM),
+    )
     return (schur, averaged, inner[0, 0])
 
 

time: 47.2 us -> 41.2 us (0.87)
  local copies, waits for them, and re-layouts: 2.29 us -> 0 us
  Pallas kernels: 42.4 us -> 40.3 us
  between operations: 2.33 us -> 0.64 us
    pallas_call x1, Pallas kernels: 42.4 us -> 38.1 us  [local(): pl.pallas_call(functools.partial(kernel, masks, groups), name='deluxe', o...]
    unnamed x2 -> x0, local copies, waits for them, and re-layouts: 2.29 us -> none
    pallas_call x0 -> x1, Pallas kernels: none -> 2.2 us  [local(): pl.pallas_call(copy_out, name='copy_out', out_shape=(jax.ShapeDtypeStruct...]
where the time goes in v3:
time: 41.2 us; the launch traced here: 41 us
  Pallas kernels  40.3 us (98%)
  between operations  0.64 us (2%)
    pallas_call x1, Pallas kernels, local(): pl.pallas_call(functools.partial(kernel, masks, groups), name='deluxe', o...  38.1 us
    pallas_call x1, Pallas kernels, local(): pl.pallas_call(copy_out, name='copy_out', out_shape=(jax.ShapeDtypeStruct...  2.2 us

profile of v3, /device:TPU:1, one launch (start us, length us, event | category | flops | bytes accessed | tf_op | source)
XLA Modules:
  0.0 41.0 jit_solution(15051261575109538456)
XLA Ops:
  0.6 38.1 %deluxe.1 = (f32[512,512]{1,0:T(8,128)S(1)}, f32[512,1024]{1,0:T(8,128)S(1)}, f32[1,1]{1,0:T(1,128)S(4)}) custom-call(bf16[2048,2048]{1,0:T(8,128)(2,1)} %inv_hbm.1, bf16[2048,512]{1,0:T(8,128)(2,1)} %cpl_hbm.1, f32[512,512]{1,0:T(8,128)} %bnd_hbm.1, f32[512,1024]{1,0:T(8,128)} %res_hbm.1, s32[1,4]{1,0:T(1,128)} %size_ref.1, f32[1,4]{1,0:T(1,128)} %scale_ref.1), custom_call_target="tpu_custom_call" | custom-call | tf_op jit(solution)/shard_map/deluxe/pallas_call | solution.py:385
  38.8 2.2 %copy_out.1 = (f32[512,512]{1,0:T(8,128)}, f32[512,1024]{1,0:T(8,128)}, f32[1,1]{1,0:T(1,128)}) custom-call(f32[512,512]{1,0:T(8,128)S(1)} %get-tuple-element.9.schur_ref, f32[512,1024]{1,0:T(8,128)S(1)} %get-tuple-element.10.avg_ref, f32[1,1]{1,0:T(1,128)S(4)} %get-tuple-element.11.inner_ref), custom_call_target="tpu_custom_call" | custom-call | tf_op jit(solution)/shard_map/copy_out/pallas_call | solution.py:421

commit v4 on v3

--- a/solution.py
+++ b/solution.py
@@ -100,6 +100,7 @@
     oth,
     own_b,
     oth_b,
+    val,
     face,
     wbuf,
     red,
@@ -111,6 +112,7 @@
     rb_sem,
     sr_sem,
     rr_sem,
+    hello_sem,
 ):
     me = lax.axis_index("sub")
     faces = len(masks)
@@ -121,9 +123,7 @@
     load_res = pltpu.make_async_copy(res_hbm, res, in_sem.at[0])
     load_res.start()
     mates = [flip(me, mask) for mask in masks]
-    peers = []
-    for group in groups:
-        peers += [flips(me, group, which) for which in range(1, 1 << len(group))]
+    peers = [flip(me, mask) for group in groups for mask in group]
     barrier = pltpu.get_barrier_semaphore()
     for peer in peers:
         pl.semaphore_signal(barrier, inc=1, device_id=(peer,), device_id_type=MESH)
@@ -168,23 +168,35 @@
         for k in range(CHUNKS)
     ]
 
-    def issue(k):
+    def issue(k, part=0):
         for r in range(faces):
-            copies[k][r].start()
+            if part == 0 or r % 2 == part - 1:
+                copies[k][r].start()
 
     rows = lax.broadcasted_iota(jnp.int32, (FMAX, width), 0)
 
+    def greet(stage):
+        for peer in peers:
+            pl.semaphore_signal(
+                hello_sem.at[stage], inc=1, device_id=(peer,), device_id_type=MESH
+            )
+
+    def greeted(stage):
+        pl.semaphore_wait(hello_sem.at[stage], len(peers))
+
+    def column(k):
+        return pl.multiple_of(((1 - odd) * k + odd * (CHUNKS - 1 - k)) * width, width)
+
     def extract(k):
-        c = (1 - odd) * k + odd * (CHUNKS - 1 - k)
-        at = pl.multiple_of(c * width, width)
         for r in range(faces):
-            piece = rows_at(res, starts[r], pl.ds(at, width))
+            piece = rows_at(res, starts[r], pl.ds(column(k), width))
             own[k, r] = jnp.where(rows < sizes[r], piece, 0.0)
 
     extract(0)
     extract(1)
     pl.semaphore_wait(barrier, len(peers))
     issue(0)
+    greet(0)
     load_cpl.wait()
     steps = ni // MROWS
     for i in range(steps):
@@ -198,6 +210,8 @@
             issue(i + 1)
     for k in range(steps + 2, CHUNKS):
         extract(k)
+    greeted(0)
+    greet(1)
     load_bnd.wait()
     schur_ref[...] = bnd[...] - lax.dot_general(
         cpl[...], sol[...], (((0,), (0,)), ((), ())), preferred_element_type=jnp.float32
@@ -231,6 +245,8 @@
         copy.start()
     for k in range(EARLY, HALF + 2):
         issue(k)
+    greeted(1)
+    greet(2)
 
     es, xs = [], []
     for r in range(faces):
@@ -267,9 +283,8 @@
         t = fold(t * t)
         partial = partial + jnp.where(row8 + a >= starts[faces], t, 0.0)
 
-    def finish(ks):
+    def average(ks):
         pair = jnp.zeros((8, 128), jnp.float32)
-        values = []
         for r in range(faces):
             for k in ks:
                 copies[k][r].wait_recv()
@@ -277,30 +292,27 @@
             ph, pw = halves(jnp.concatenate(both, axis=1))
             top = mm(wbuf[r], ph)
             value = top[:FMAX] + top[FMAX:] + mm(wbuf[r, pl.ds(0, FMAX), :], pw)
-            values.append(value)
             for j, k in enumerate(ks):
+                part = value[:, j * width : (j + 1) * width]
+                val[k, r] = part
                 if k < HALF:
-                    part = value[:, j * width : (j + 1) * width]
                     pair = pair + fold((both[j][:FMAX] + both[j][FMAX:]) * part)
-        for j, k in enumerate(ks):
-            c = odd * k + (1 - odd) * (CHUNKS - 1 - k)
-            at = pl.multiple_of(c * width, width)
+        return pair
+
+    def place(k):
+        at = column(CHUNKS - 1 - k)
+        for r in range(faces):
+            face[k % 2, pl.ds(r * SPAN, SPAN), :] = rows_down(val[k, r], starts[r] - whole[r])
+        here = lax.broadcasted_iota(jnp.int32, (8, width), 0)
+        for a in range(0, nb, 8):
+            t = res[pl.ds(a, 8), pl.ds(at, width)]
             for r in range(faces):
-                part = values[r][:, j * width : (j + 1) * width]
-                face[k % 2, pl.ds(r * SPAN, SPAN), :] = rows_down(part, starts[r] - whole[r])
-            here = lax.broadcasted_iota(jnp.int32, (8, width), 0)
-            for a in range(0, nb, 8):
-                t = res[pl.ds(a, 8), pl.ds(at, width)]
-                for r in range(faces):
-                    if a >= r * (FMAX // 2) and a < (r + 1) * FMAX:
-                        tile = a // 8 + r * (SPAN // 8) - lax.div(starts[r], 8)
-                        tile = jnp.clip(tile, 0, face.shape[1] // 8 - 1)
-                        shifted = face[k % 2, pl.ds(tile * 8, 8), :]
-                        t = jnp.where(
-                            (here >= starts[r] - a) & (here < starts[r + 1] - a), shifted, t
-                        )
-                avg_ref[pl.ds(a, 8), pl.ds(at, width)] = t
-        return pair
+                if a >= r * (FMAX // 2) and a < (r + 1) * FMAX:
+                    tile = a // 8 + r * (SPAN // 8) - lax.div(starts[r], 8)
+                    tile = jnp.clip(tile, 0, face.shape[1] // 8 - 1)
+                    shifted = face[k % 2, pl.ds(tile * 8, 8), :]
+                    t = jnp.where((here >= starts[r] - a) & (here < starts[r + 1] - a), shifted, t)
+            avg_ref[pl.ds(a, 8), pl.ds(at, width)] = t
 
     bases = [0]
     for group in groups:
@@ -332,19 +344,27 @@
             total = total + red[j]
         return total
 
-    for k in range(0, HALF, 2):
-        partial = partial + finish((k, k + 1))
+    for ks in ((0, 1), (2, 3)):
+        partial = partial + average(ks)
     partial = jnp.sum(partial, axis=0, keepdims=True)
-    sends = []
-    for g in range(len(groups)):
-        round_copies = spread(g, partial)
-        sends += round_copies
-        if HALF + 2 + g < CHUNKS:
-            issue(HALF + 2 + g)
-        finish((HALF + g,))
-        partial = gather(g, round_copies)
-    for k in range(HALF + len(groups), CHUNKS):
-        finish((k,))
+    greeted(2)
+    sends = spread(0, partial)
+    issue(6)
+    for k in range(HALF):
+        place(k)
+    average((4,))
+    place(4)
+    partial = gather(0, sends)
+    last = spread(1, partial)
+    sends += last
+    issue(7)
+    average((5,))
+    place(5)
+    average((6,))
+    place(6)
+    average((7,))
+    place(7)
+    partial = gather(1, last)
     inner_ref[0, 0] = jnp.sum(partial)
 
     for copy in sends:
@@ -402,6 +422,7 @@
             pltpu.VMEM((CHUNKS, faces, FMAX, width), f32),
             pltpu.VMEM((faces, FMAX, FMAX), f32),
             pltpu.VMEM((faces, FMAX, FMAX), f32),
+            pltpu.VMEM((CHUNKS, faces, FMAX, width), f32),
             pltpu.VMEM((2, faces * SPAN + (faces - 1) * (FMAX // 2) - 8, width), f32),
             pltpu.VMEM((faces, 2 * FMAX, 2 * FMAX), bf16),
             pltpu.VMEM((slots, 1, 128), f32),
@@ -413,6 +434,7 @@
             dma((faces,)),
             dma((slots,)),
             dma((slots,)),
+            pltpu.SemaphoreType.REGULAR((3,)),
         ],
         compiler_params=pltpu.CompilerParams(
             collective_id=0, has_side_effects=True, vmem_limit_bytes=56 * 2**20

time: 41.2 us -> 39.1 us (0.949)
  Pallas kernels: 40.3 us -> 38.2 us
    pallas_call x1, Pallas kernels: 38.1 us -> 36 us  [local(): pl.pallas_call(functools.partial(kernel, masks, groups), name='deluxe', o...]
where the time goes in v4:
time: 39.1 us; the launch traced here: 38.8 us
  Pallas kernels  38.2 us (98%)
  between operations  0.64 us (2%)
    pallas_call x1, Pallas kernels, local(): pl.pallas_call(functools.partial(kernel, masks, groups), name='deluxe', o...  36 us
    pallas_call x1, Pallas kernels, local(): pl.pallas_call(copy_out, name='copy_out', out_shape=(jax.ShapeDtypeStruct...  2.2 us

profile of v4, /device:TPU:1, one launch (start us, length us, event | category | flops | bytes accessed | tf_op | source)
XLA Modules:
  0.0 38.8 jit_solution(18045349760953774053)
XLA Ops:
  0.6 36.0 %deluxe.1 = (f32[512,512]{1,0:T(8,128)S(1)}, f32[512,1024]{1,0:T(8,128)S(1)}, f32[1,1]{1,0:T(1,128)S(4)}) custom-call(bf16[2048,2048]{1,0:T(8,128)(2,1)} %inv_hbm.1, bf16[2048,512]{1,0:T(8,128)(2,1)} %cpl_hbm.1, f32[512,512]{1,0:T(8,128)} %bnd_hbm.1, f32[512,1024]{1,0:T(8,128)} %res_hbm.1, s32[1,4]{1,0:T(1,128)} %size_ref.1, f32[1,4]{1,0:T(1,128)} %scale_ref.1), custom_call_target="tpu_custom_call" | custom-call | tf_op jit(solution)/shard_map/deluxe/pallas_call | solution.py:405
  36.6 2.2 %copy_out.1 = (f32[512,512]{1,0:T(8,128)}, f32[512,1024]{1,0:T(8,128)}, f32[1,1]{1,0:T(1,128)}) custom-call(f32[512,512]{1,0:T(8,128)S(1)} %get-tuple-element.9.schur_ref, f32[512,1024]{1,0:T(8,128)S(1)} %get-tuple-element.10.avg_ref, f32[1,1]{1,0:T(1,128)S(4)} %get-tuple-element.11.inner_ref), custom_call_target="tpu_custom_call" | custom-call | tf_op jit(solution)/shard_map/copy_out/pallas_call | solution.py:443

commit v5 on v4

--- a/solution.py
+++ b/solution.py
@@ -86,11 +86,14 @@
     cpl_hbm,
     bnd_hbm,
     res_hbm,
-    size_ref,
-    scale_ref,
+    size_hbm,
+    scale_hbm,
     schur_ref,
     avg_ref,
     inner_ref,
+    size_ref,
+    scale_ref,
+    small_sem,
     inv,
     cpl,
     sol,
@@ -120,38 +123,34 @@
     columns = res.shape[1]
     width = columns // CHUNKS
 
-    load_res = pltpu.make_async_copy(res_hbm, res, in_sem.at[0])
-    load_res.start()
     mates = [flip(me, mask) for mask in masks]
     peers = [flip(me, mask) for group in groups for mask in group]
     barrier = pltpu.get_barrier_semaphore()
     for peer in peers:
         pl.semaphore_signal(barrier, inc=1, device_id=(peer,), device_id_type=MESH)
 
+    load_size = pltpu.make_async_copy(size_hbm, size_ref, small_sem.at[0])
+    load_size.start()
+    load_scale = pltpu.make_async_copy(scale_hbm, scale_ref, small_sem.at[1])
+    load_scale.start()
     odd = 0
     for mask in masks:
         odd = odd + (me // mask) % 2
     odd = odd % 2
+
+    def column(k):
+        return pl.multiple_of(((1 - odd) * k + odd * (CHUNKS - 1 - k)) * width, width)
+
+    load_res = pltpu.make_async_copy(res_hbm, res, in_sem.at[0])
+    load_res.start()
+    load_size.wait()
+    load_scale.wait()
     sizes = [size_ref[0, r] for r in range(faces)]
     starts = [jnp.int32(0)]
     for r in range(faces):
         starts.append(starts[-1] + sizes[r])
     whole = [lax.div(start, 8) * 8 for start in starts]
     face[...] = jnp.zeros_like(face)
-
-    load_res.wait()
-    load_cpl = pltpu.make_async_copy(cpl_hbm, cpl, in_sem.at[1])
-    load_cpl.start()
-    load_inv = [
-        pltpu.make_async_copy(
-            inv_hbm.at[pl.ds(i * MROWS, MROWS)], inv.at[pl.ds(i * MROWS, MROWS)], inv_sem.at[i]
-        )
-        for i in range(ni // MROWS)
-    ]
-    for copy in load_inv:
-        copy.start()
-    load_bnd = pltpu.make_async_copy(bnd_hbm, bnd, in_sem.at[2])
-    load_bnd.start()
 
     copies = [
         [
@@ -184,18 +183,28 @@
     def greeted(stage):
         pl.semaphore_wait(hello_sem.at[stage], len(peers))
 
-    def column(k):
-        return pl.multiple_of(((1 - odd) * k + odd * (CHUNKS - 1 - k)) * width, width)
-
     def extract(k):
         for r in range(faces):
             piece = rows_at(res, starts[r], pl.ds(column(k), width))
             own[k, r] = jnp.where(rows < sizes[r], piece, 0.0)
 
+    load_res.wait()
     extract(0)
-    extract(1)
+    load_cpl = pltpu.make_async_copy(cpl_hbm, cpl, in_sem.at[1])
+    load_cpl.start()
+    load_inv = [
+        pltpu.make_async_copy(
+            inv_hbm.at[pl.ds(i * MROWS, MROWS)], inv.at[pl.ds(i * MROWS, MROWS)], inv_sem.at[i]
+        )
+        for i in range(ni // MROWS)
+    ]
+    for copy in load_inv:
+        copy.start()
+    load_bnd = pltpu.make_async_copy(bnd_hbm, bnd, in_sem.at[2])
+    load_bnd.start()
     pl.semaphore_wait(barrier, len(peers))
     issue(0)
+    extract(1)
     greet(0)
     load_cpl.wait()
     steps = ni // MROWS
@@ -219,6 +228,17 @@
 
     i0 = lax.broadcasted_iota(jnp.int32, (FMAX, FMAX), 0)
     i1 = lax.broadcasted_iota(jnp.int32, (FMAX, FMAX), 1)
+    block_copies = [
+        pltpu.make_async_remote_copy(
+            src_ref=own_b.at[r],
+            dst_ref=oth_b.at[r],
+            send_sem=sb_sem.at[r],
+            recv_sem=rb_sem.at[r],
+            device_id=(mates[r],),
+            device_id_type=MESH,
+        )
+        for r in range(faces)
+    ]
     for r in range(faces):
         left = jnp.minimum(lax.div(starts[r], FMAX), nb // FMAX - 2) * FMAX
         band = rows_at(schur_ref, starts[r], pl.ds(left, 2 * FMAX))
@@ -230,19 +250,9 @@
         parts = mm(jnp.concatenate([hi, lo, rest.astype(jnp.bfloat16)], axis=0), pick)
         block = parts[:FMAX] + parts[FMAX : 2 * FMAX] + parts[2 * FMAX :]
         own_b[r] = jnp.where((i0 < sizes[r]) & (i1 < sizes[r]), block, 0.0)
-    block_copies = [
-        pltpu.make_async_remote_copy(
-            src_ref=own_b.at[r],
-            dst_ref=oth_b.at[r],
-            send_sem=sb_sem.at[r],
-            recv_sem=rb_sem.at[r],
-            device_id=(mates[r],),
-            device_id_type=MESH,
-        )
-        for r in range(faces)
-    ]
-    for copy in block_copies:
-        copy.start()
+        if r > 0:
+            block_copies[r - 1].start()
+    block_copies[faces - 1].start()
     for k in range(EARLY, HALF + 2):
         issue(k)
     greeted(1)
@@ -380,10 +390,10 @@
     copies = [
         pltpu.make_async_copy(avg_ref, avg_out, sem.at[0]),
         pltpu.make_async_copy(schur_ref, schur_out, sem.at[1]),
+        pltpu.make_async_copy(inner_ref, inner_out, sem.at[2]),
     ]
     for copy in copies:
         copy.start()
-    inner_out[0, 0] = inner_ref[0, 0]
     for copy in copies:
         copy.wait()
 
@@ -410,9 +420,12 @@
             pltpu.VMEM((nb, columns), f32),
             pltpu.SMEM((1, 1), f32),
         ),
-        in_specs=[anyspec, anyspec, anyspec, anyspec, smem, smem],
+        in_specs=[anyspec] * 6,
         out_specs=(vmem, vmem, smem),
         scratch_shapes=[
+            pltpu.SMEM((1, faces), jnp.int32),
+            pltpu.SMEM((1, faces), f32),
+            dma((2,)),
             pltpu.VMEM((ni, ni), bf16),
             pltpu.VMEM((ni, nb), bf16),
             pltpu.VMEM((ni, nb), bf16),
@@ -449,8 +462,8 @@
             jax.ShapeDtypeStruct((1, 1), f32),
         ),
         in_specs=[vmem, vmem, smem],
-        out_specs=(anyspec, anyspec, smem),
-        scratch_shapes=[dma((2,))],
+        out_specs=(anyspec, anyspec, anyspec),
+        scratch_shapes=[dma((3,))],
     )(
         pltpu.with_memory_space_constraint(schur, pltpu.VMEM),
         pltpu.with_memory_space_constraint(averaged, pltpu.VMEM),

time: 39.1 us -> 38.1 us (0.974)
  Pallas kernels: 38.2 us -> 37.2 us
    pallas_call x1, Pallas kernels: 36 us -> 35.5 us  [local(): pl.pallas_call(functools.partial(kernel, masks, groups), name='deluxe', o...]
    pallas_call x1, Pallas kernels: 2.2 us -> 1.7 us  [local(): pl.pallas_call(copy_out, name='copy_out', out_shape=(jax.ShapeDtypeStruct...]
where the time goes in v5:
time: 38.1 us; the launch traced here: 37.8 us
  Pallas kernels  37.2 us (98%)
  between operations  0.64 us (2%)
    pallas_call x1, Pallas kernels, local(): pl.pallas_call(functools.partial(kernel, masks, groups), name='deluxe', o...  35.5 us
    pallas_call x1, Pallas kernels, local(): pl.pallas_call(copy_out, name='copy_out', out_shape=(jax.ShapeDtypeStruct...  1.7 us

profile of v5, /device:TPU:1, one launch (start us, length us, event | category | flops | bytes accessed | tf_op | source)
XLA Modules:
  0.0 37.8 jit_solution(2309925303560531173)
XLA Ops:
  0.6 35.5 %deluxe.1 = (f32[512,512]{1,0:T(8,128)S(1)}, f32[512,1024]{1,0:T(8,128)S(1)}, f32[1,1]{1,0:T(1,128)S(4)}) custom-call(bf16[2048,2048]{1,0:T(8,128)(2,1)} %inv_hbm.1, bf16[2048,512]{1,0:T(8,128)(2,1)} %cpl_hbm.1, f32[512,512]{1,0:T(8,128)} %bnd_hbm.1, f32[512,1024]{1,0:T(8,128)} %res_hbm.1, s32[1,4]{1,0:T(1,128)} %size_hbm.1, f32[1,4]{1,0:T(1,128)} %scale_hbm.1), custom_call_target="tpu_custom_call" | custom-call | tf_op jit(solution)/shard_map/deluxe/pallas_call | solution.py:415
  36.1 1.7 %copy_out.1 = (f32[512,512]{1,0:T(8,128)}, f32[512,1024]{1,0:T(8,128)}, f32[1,1]{1,0:T(1,128)}) custom-call(f32[512,512]{1,0:T(8,128)S(1)} %get-tuple-element.9.schur_ref, f32[512,1024]{1,0:T(8,128)S(1)} %get-tuple-element.10.avg_ref, f32[1,1]{1,0:T(1,128)S(4)} %get-tuple-element.11.inner_ref), custom_call_target="tpu_custom_call" | custom-call | tf_op jit(solution)/shard_map/copy_out/pallas_call | solution.py:456

commit v6 on v5

--- a/solution.py
+++ b/solution.py
@@ -150,7 +150,6 @@
     for r in range(faces):
         starts.append(starts[-1] + sizes[r])
     whole = [lax.div(start, 8) * 8 for start in starts]
-    face[...] = jnp.zeros_like(face)
 
     copies = [
         [
@@ -205,20 +204,19 @@
     pl.semaphore_wait(barrier, len(peers))
     issue(0)
     extract(1)
+    face[...] = jnp.zeros_like(face)
     greet(0)
     load_cpl.wait()
     steps = ni // MROWS
     for i in range(steps):
         load_inv[i].wait()
-        if i + 2 < CHUNKS:
+        if i + 2 <= EARLY:
             extract(i + 2)
         sol[pl.ds(i * MROWS, MROWS), :] = mm(inv[pl.ds(i * MROWS, MROWS), :], cpl[...]).astype(
             jnp.bfloat16
         )
         if i + 1 < EARLY:
             issue(i + 1)
-    for k in range(steps + 2, CHUNKS):
-        extract(k)
     greeted(0)
     greet(1)
     load_bnd.wait()
@@ -253,8 +251,11 @@
         if r > 0:
             block_copies[r - 1].start()
     block_copies[faces - 1].start()
-    for k in range(EARLY, HALF + 2):
-        issue(k)
+    issue(EARLY)
+    for k in range(EARLY + 1, CHUNKS):
+        extract(k)
+        if EARLY + 1 < k <= HALF + 2:
+            issue(k - 1)
     greeted(1)
     greet(2)
 

time: 38.1 us -> 37.8 us (level)
  no operation moved by 1% of the time
where the time goes in v6:
time: 37.8 us; the launch traced here: 37.5 us
  Pallas kernels  36.9 us (98%)
  between operations  0.64 us (2%)
    pallas_call x1, Pallas kernels, local(): pl.pallas_call(functools.partial(kernel, masks, groups), name='deluxe', o...  35.2 us
    pallas_call x1, Pallas kernels, local(): pl.pallas_call(copy_out, name='copy_out', out_shape=(jax.ShapeDtypeStruct...  1.7 us

profile of v6, /device:TPU:1, one launch (start us, length us, event | category | flops | bytes accessed | tf_op | source)
XLA Modules:
  0.0 37.5 jit_solution(5464522294492714924)
XLA Ops:
  0.6 35.2 %deluxe.1 = (f32[512,512]{1,0:T(8,128)S(1)}, f32[512,1024]{1,0:T(8,128)S(1)}, f32[1,1]{1,0:T(1,128)S(4)}) custom-call(bf16[2048,2048]{1,0:T(8,128)(2,1)} %inv_hbm.1, bf16[2048,512]{1,0:T(8,128)(2,1)} %cpl_hbm.1, f32[512,512]{1,0:T(8,128)} %bnd_hbm.1, f32[512,1024]{1,0:T(8,128)} %res_hbm.1, s32[1,4]{1,0:T(1,128)} %size_hbm.1, f32[1,4]{1,0:T(1,128)} %scale_hbm.1), custom_call_target="tpu_custom_call" | custom-call | tf_op jit(solution)/shard_map/deluxe/pallas_call | solution.py:416
  35.8 1.7 %copy_out.1 = (f32[512,512]{1,0:T(8,128)}, f32[512,1024]{1,0:T(8,128)}, f32[1,1]{1,0:T(1,128)}) custom-call(f32[512,512]{1,0:T(8,128)S(1)} %get-tuple-element.9.schur_ref, f32[512,1024]{1,0:T(8,128)S(1)} %get-tuple-element.10.avg_ref, f32[1,1]{1,0:T(1,128)S(4)} %get-tuple-element.11.inner_ref), custom_call_target="tpu_custom_call" | custom-call | tf_op jit(solution)/shard_map/copy_out/pallas_call | solution.py:457
